TPU v7x, 256 devices: a whole 4x4x8 slice. The times are simulated.
256 devices in a mesh: ka: 4 (over z_hi, core), fit: 64 (over x, y, z_lo).
Axes of the slice: x: 4, y: 4, z: 8 (z_hi: 2, z_lo: 4; z = z_hi * 4 + z_lo), core: 2. Of those that a mesh axis runs over, the one named last changes fastest.
Arguments:
- integrals: bfloat16 [3, 4, 64, 48, 64, 128], P(None, 'ka', 'fit'), may hold values from -0.3125 to 0.3125
- block_lists: int32 [3, 4, 64, 2, 48], P(None, 'ka', 'fit'), may hold values from 0 to 15, as said below
- coeff: bfloat16 [4, 2, 1024, 256], P('ka', None, 'fit'), may hold values from -6 to 6
- match: int32 [3, 4], replicated, may hold values from 0 to 3, each once within a row
- ex_blocks: int32 [4, 2, 64], P('ka'), may hold values from 0 to 15, as said below
Outputs:
- exchange: float32 [4, 4096, 128], P('ka', 'fit')
Inputs may be any that keep to these rules, and one draw needn't show every extreme that they name: `block_lists`: each integral matrix lists 48 distinct blocks; each entry is a block index below 16, row first then column. `ex_blocks`: each k-point lists 64 distinct blocks, none on the diagonal (row block differs from column block).
All inputs are finite; a program needn't handle non-finite values.
Results may differ from a plain program's by a relative error of at most 0.0036.
Values may be sent and summed in bfloat16 or wider, within the bound.
A program may use at most 128 MiB of HBM per device.

v0:
```python
import jax
import jax.numpy as jnp
from jax import lax
from jax.sharding import PartitionSpec as P


def block_operands(coeff_one, edge):
    nblocks = coeff_one.shape[1] // edge
    real = coeff_one[0].reshape(nblocks, edge, -1)
    imag = coeff_one[1].reshape(nblocks, edge, -1)
    upper = jnp.concatenate([real, imag], axis=2)
    lower = jnp.concatenate([-imag, real], axis=2)
    return jnp.concatenate([upper, lower], axis=1)


def half_transform(lmat, lists, operands):
    nblocks = operands.shape[0]
    picked = jnp.take(operands, lists[1], axis=0)
    prods = jnp.einsum("bmi,bij->bmj", lmat, picked, preferred_element_type=jnp.float32)
    onehot = (lists[0][None, :] == jnp.arange(nblocks, dtype=jnp.int32)[:, None]).astype(
        jnp.float32
    )
    rows = jnp.einsum("rb,bmj->rmj", onehot, prods, precision=lax.Precision.HIGHEST)
    return rows.astype(jnp.bfloat16)


def exchange_blocks(xmat, listed):
    occ = xmat.shape[2] // 2
    left = jnp.take(xmat, listed[0], axis=0)
    right = jnp.take(xmat, listed[1], axis=0)
    swapped = jnp.concatenate([left[:, :, occ:], -left[:, :, :occ]], axis=2)
    kreal = jnp.einsum("emj,enj->emn", left, right, preferred_element_type=jnp.float32)
    kimag = jnp.einsum("emj,enj->emn", swapped, right, preferred_element_type=jnp.float32)
    return jnp.concatenate([kreal, kimag], axis=2)


def on_device(integrals, block_lists, coeff, match, ex_blocks):
    kdev = coeff.shape[0]
    nq = integrals.shape[0]
    adev = integrals.shape[2]
    edge = integrals.shape[4]
    occ = coeff.shape[3]
    nexch = ex_blocks.shape[2]
    naux = adev * lax.axis_size("fit")
    factor = -((nq * naux * occ) ** (-0.5))
    kglob = lax.axis_index("ka") * kdev + jnp.arange(kdev, dtype=jnp.int32)
    shards = lax.all_gather(coeff, "ka", axis=0, tiled=True)
    pending = jnp.zeros((kdev, nexch * edge, 2 * edge), jnp.float32)
    total = None
    for qq in range(nq):
        partner = jnp.take(match[qq], kglob, axis=0)
        partner_full = lax.all_gather(jnp.take(shards, partner, axis=0), "fit", axis=2, tiled=True)
        operands = block_operands(partner_full[0], edge)
        xmat = half_transform(integrals[qq, 0, 0], block_lists[qq, 0, 0], operands)
        summed = exchange_blocks(xmat, ex_blocks[0])
        blocks_all = [summed]
        flat = (jnp.stack(blocks_all) * factor).reshape(kdev, nexch * edge, 2 * edge)
        pending = pending + flat
    whole = lax.psum(pending, "fit")
    share = whole.shape[1] // lax.axis_size("fit")
    total = lax.dynamic_slice_in_dim(whole, lax.axis_index("fit") * share, share, 1)
    return total


def solution(mesh):
    return jax.shard_map(
        on_device,
        mesh=mesh,
        in_specs=(
            P(None, "ka", "fit", None, None, None),
            P(None, "ka", "fit", None, None),
            P("ka", None, "fit", None),
            P(),
            P("ka", None, None),
        ),
        out_specs=P("ka", "fit", None),
        check_vma=False,
    )
```

profile of v0, /device:TPU:8, one launch (start us, length us, event | category | flops | bytes accessed | tf_op | source)
XLA Modules:
  0.0 1848.3 jit_solution(7708082397937562943)
XLA Ops:
  6.5 0.0 all-gather.6.cloned.1.call-start
  6.5 0.8 fusion.86
  7.3 0.7 fusion.87
  11.9 0.6 fusion.89
  14.4 10.7 all_gather.12
  25.0 0.6 dynamic-slice_select_fusion
  25.7 0.0 all-gather.6.cloned.1.call-update
  25.7 0.0 all-gather.4.cloned.1.call-start
  25.7 0.7 all-gather.4.cloned.1.call-update
  26.4 0.0 all-gather.8.cloned.1.call-start
  26.5 0.7 all-gather.8.cloned.1.call-update
  27.2 0.0 all-reduce.2.cloned.1.call-start
  27.2 0.7 compare_and_fusion
  28.0 0.7 slice_bitcast_fusion
  28.7 0.8 compare_and_fusion.2
  29.5 340.9 %all-gather.6.cloned.1.call-done = bf16[1,2,1024,256]{3,2,1,0:T(8,128)(2,1)} async-done(((bf16[1,2,16,256]{3,2,1,0:T(8,128)(2,1)}), bf16[1,2,1024,256]{3,2,1,0:T(8,128)(2,1)}) %all-gather.6.cloned.1.call-update) | async-done | bytes 1048592 | tf_op jit(solution)/shard_map/all_gather | solution.py:52
  370.4 1.3 fusion.84
  371.7 0.1 neg.20
  371.8 0.2 maximum_maximum_fusion.1
  372.0 4.9 gather_fusion.3
  376.9 4.3 fusion.33
  381.2 5.7 fusion.47
  387.0 0.6 copy.28
  387.6 330.7 %all-gather.4.cloned.1.call-done = bf16[1,2,1024,256]{3,2,1,0:T(8,128)(2,1)} async-done(((bf16[1,2,16,256]{3,2,1,0:T(8,128)(2,1)}), bf16[1,2,1024,256]{3,2,1,0:T(8,128)(2,1)}) %all-gather.4.cloned.1.call-update) | async-done | bytes 1048592 | tf_op jit(solution)/shard_map/all_gather | solution.py:52
  718.3 1.3 fusion.85
  719.6 0.1 neg.18
  719.7 0.2 maximum_maximum_fusion
  719.9 5.4 gather_fusion
  725.3 4.3 fusion.30
  729.6 5.7 fusion.44
  735.3 0.6 copy.25
  735.9 2.8 gather_fusion.4
  738.7 2.8 gather_fusion.1
  741.5 2.9 gather_fusion.2
  744.4 2.9 gather_fusion.5
  747.3 318.9 %all-gather.8.cloned.1.call-done = bf16[1,2,1024,256]{3,2,1,0:T(8,128)(2,1)} async-done(((bf16[1,2,16,256]{3,2,1,0:T(8,128)(2,1)}), bf16[1,2,1024,256]{3,2,1,0:T(8,128)(2,1)}) %all-gather.8.cloned.1.call-update) | async-done | bytes 1048592 | tf_op jit(solution)/shard_map/all_gather | solution.py:52
  1066.2 1.3 fusion.83
  1067.5 0.1 neg.22
  1067.6 0.2 maximum_maximum_fusion.2
  1067.8 5.1 gather_fusion.6
  1072.8 4.3 fusion.36
  1077.2 5.7 fusion.50
  1082.9 0.6 copy.31
  1083.5 2.9 gather_fusion.7
  1086.4 2.8 gather_fusion.8
  1089.1 5.5 broadcast_select_fusion.3
  1094.7 2.3 fusion.82
  1096.9 0.0 copy-start.1
  1096.9 0.3 fusion.81
  1097.2 1.9 copy-done.1
  1099.1 1.3 fusion.41
  1100.4 0.9 copy-done
  1101.3 1.3 fusion.42
  1102.6 0.0 copy-start.2
  1102.6 2.4 fusion.80
  1105.0 1.3 copy-done.2
  1106.3 1.3 fusion.43
  1107.7 3.1 fusion.15
  1110.8 1.6 fusion.19
  1112.5 3.1 fusion.23
  1115.6 3.0 fusion.40
  1118.6 0.0 all-reduce.2.cloned.1.call-update
  1118.6 721.5 %all-reduce.2.cloned.1.call-done = f32[1,4096,128]{2,1,0:T(8,128)} async-done(((f32[1,4096,128]{2,1,0:T(8,128)}), f32[1,4096,128]{2,1,0:T(8,128)}) %all-reduce.2.cloned.1.call-update) | async-done | bytes 2097168 | tf_op jit(solution)/shard_map/psum | solution.py:59
  1840.1 1.4 constant_dynamic-slice_fusion.3
  (4 shorter events, 0.0 us)
Async XLA Ops:
  6.5 363.9 %all-gather.6.cloned.1.call-start = ((), (), s32[]{:S(2)}) async-start(), calls=%async_computation.1 | async-start | bytes 1064960 | tf_op jit(solution)/shard_map/all_gather | solution.py:52
  25.7 692.6 %all-gather.4.cloned.1.call-start = ((), (), s32[]{:S(2)}) async-start(), calls=%async_computation | async-start | bytes 1064960 | tf_op jit(solution)/shard_map/all_gather | solution.py:52
  26.4 1039.8 %all-gather.8.cloned.1.call-start = ((), (), s32[]{:S(2)}) async-start(), calls=%async_computation.2 | async-start | bytes 1064960 | tf_op jit(solution)/shard_map/all_gather | solution.py:52
  27.2 1813.0 %all-reduce.2.cloned.1.call-start = ((), (), s32[]{:S(2)}) async-start(), calls=%async_computation.3 | async-start | bytes 4194304 | tf_op jit(solution)/shard_map/psum | solution.py:59
  1096.9 2.2 copy-start.1
  1099.1 2.2 copy-start
  1102.6 3.7 copy-start.2
Sparse Core Ops, SparseCore 0:
  25.8 344.5 all-gather.5
  372.2 346.0 all-gather.3
  720.1 346.0 all-gather.7
  1118.8 721.3 all-reduce.1
where the time goes:
time: 1860 us; the launch traced here: 1850 us
  waiting for transfers between devices  1710 us (92%)
  local copies, waits for them, and re-layouts  44.9 us (2%)
  matrix products  42.1 us (2%)
  between operations  19.3 us (1%)
    all_gather x3, waiting for transfers between devices, on_device(): lax.all_gather(jnp.take(shards, partner, axis=0), 'fit', axis=2, tiled=True)  991 us
    psum x1, waiting for transfers between devices, on_device(): whole = lax.psum(pending, 'fit')  721 us
  transfers between devices with their start and end apart: 4, of which 4 were waited for; matrix products, arithmetic and copies ran while one was open for 3% of the time, Pallas kernels for 0%

commit v1 on v0

v1 whole, which is shorter than its diff:
```python
import jax
import jax.numpy as jnp
from jax import lax
from jax.experimental import pallas as pl
from jax.experimental.pallas import tpu as pltpu
from jax.sharding import PartitionSpec as P

MESH = pl.DeviceIdType.MESH
NT = (((1,), (1,)), ((), ()))
F32 = jnp.float32
BF16 = jnp.bfloat16


def place():
    ka, fit = lax.axis_index("ka"), lax.axis_index("fit")
    x, y, zl = fit // 16, (fit // 4) % 4, fit % 4
    return ka // 2, ka % 2, x, y, zl


def device(zh, c, x, y, zl):
    return (zh * 2 + c, x * 16 + y * 4 + zl)


def rcopy(src, dst, ssem, rsem, dev):
    return pltpu.make_async_remote_copy(
        src_ref=src, dst_ref=dst, send_sem=ssem, recv_sem=rsem, device_id=dev, device_id_type=MESH
    )


def greet(devices):
    barrier = pltpu.get_barrier_semaphore()
    for dev in devices:
        pl.semaphore_signal(barrier, inc=1, device_id=dev, device_id_type=MESH)
    pl.semaphore_wait(barrier, len(devices))


def gather_kernel(coeff, out, g, lsem, zs, zr, rs, rr, bs, br):
    zh, c, x, y, zl = place()
    z = zh * 4 + zl
    own = pl.ds(pl.multiple_of(zl * 16, 16), 16)
    loads = []
    for h in range(2):
        for s in range(2):
            cp = pltpu.make_async_copy(
                coeff.at[0, s, :, h * 128 : (h + 1) * 128], g.at[zh, c, h, s, x, y, own], lsem.at[h * 2 + s]
            )
            cp.start()
            loads.append(cp)

    def nb(dx, dy):
        return device(zh, c, (x + dx + 4) % 4, (y + dy + 4) % 4, zl)

    zdev = []
    for j in range(1, 8):
        zz = (z + j) % 8
        zdev.append(device(zz // 4, c, x, y, zz % 4))
    sib = device(zh, 1 - c, x, y, zl)
    greet(zdev + [nb(1, 0), nb(-1, 0), nb(0, 1), nb(0, -1), sib])
    for cp in loads:
        cp.wait()

    piece = g.at[zh, c, :, :, x, y, own]
    zc = [rcopy(piece, piece, zs.at[j], zr.at[j], zdev[j]) for j in range(7)]
    for cp in zc:
        cp.start()
    for cp in zc:
        cp.wait()

    started = []

    def ring(n, part, up, down, block):
        first = {}
        for i, dev in ((0, up), (1, down)):
            for s in range(2):
                cp = rcopy(block(0, s), block(0, s), rs.at[n, i, s], rr.at[n, i, s], dev)
                cp.start()
                first[i, s] = cp
        return first

    def relay(n, first, up, down, block):
        first[0, 0].wait_recv()
        a = rcopy(block(-1, 0), block(-1, 0), rs.at[n, 2, 0], rr.at[n, 2, 0], up)
        a.start()
        first[1, 1].wait_recv()
        b = rcopy(block(1, 1), block(1, 1), rs.at[n, 2, 1], rr.at[n, 2, 1], down)
        b.start()
        first[0, 1].wait_recv()
        first[1, 0].wait_recv()
        return [a, b]

    def blk_a2(d, s):
        return g.at[:, c, 0, s, x, (y + d + 4) % 4]

    def blk_b2(d, s):
        return g.at[:, c, 1, s, (x + d + 4) % 4, y]

    def blk_a3(d, s):
        return g.at[:, c, 0, s, (x + d + 4) % 4]

    def blk_b3(d, s):
        return g.at[:, c, 1, s, :, (y + d + 4) % 4]

    ax = (nb(1, 0), nb(-1, 0))
    ay = (nb(0, 1), nb(0, -1))
    fa = ring(0, 0, *ay, blk_a2)
    fb = ring(1, 1, *ax, blk_b2)
    ra = relay(0, fa, *ay, blk_a2)
    rb = relay(1, fb, *ax, blk_b2)
    for cp in ra + rb:
        cp.wait_recv()
    fa3 = ring(2, 0, *ax, blk_a3)
    fb3 = ring(3, 1, *ay, blk_b3)
    sibs = []

    def to_sib(i, block, d):
        for s in range(2):
            cp = rcopy(block(d, s), block(d, s), bs.at[i, s], br.at[i, s], sib)
            cp.start()
            sibs.append(cp)

    to_sib(0, blk_a3, 0)
    to_sib(1, blk_b3, 0)
    ra3 = relay(2, fa3, *ax, blk_a3)
    rb3 = relay(3, fb3, *ay, blk_b3)
    to_sib(2, blk_a3, 1)
    to_sib(3, blk_b3, 1)
    to_sib(4, blk_a3, -1)
    to_sib(5, blk_b3, -1)
    for cp in ra3 + rb3:
        cp.wait_recv()
    to_sib(6, blk_a3, 2)
    to_sib(7, blk_b3, 2)
    for cp in sibs:
        cp.wait()
    for f in (fa, fb, fa3, fb3):
        for cp in f.values():
            cp.wait_send()
    for cp in ra + rb + ra3 + rb3:
        cp.wait_send()
    cp = pltpu.make_async_copy(g, out, lsem.at[0])
    cp.start()
    cp.wait()


def gather(coeff):
    shape = (2, 2, 2, 2, 4, 4, 64, 128)
    dma = pltpu.SemaphoreType.DMA
    return pl.pallas_call(
        gather_kernel,
        out_shape=jax.ShapeDtypeStruct(shape, BF16),
        in_specs=[pl.BlockSpec(memory_space=pl.ANY)],
        out_specs=pl.BlockSpec(memory_space=pl.ANY),
        scratch_shapes=[
            pltpu.VMEM(shape, BF16),
            dma((4,)),
            dma((7,)),
            dma((7,)),
            dma((4, 3, 2)),
            dma((4, 3, 2)),
            dma((8, 2)),
            dma((8, 2)),
        ],
        compiler_params=pltpu.CompilerParams(collective_id=0, has_side_effects=True),
        name="gather",
    )(coeff)


def local_kernel(idx, part, ex, lin, g, sf, sb, lv, ld, xs):
    lv[0:144] = lin[...]
    lv[144] = jnp.zeros((64, 128), BF16)

    @pl.loop(0, 48)
    def _(i):
        q, c = i // 16, i % 16
        for r in range(16):
            ld[q, c, r * 64 : (r + 1) * 64, :] = lv[idx[q, r * 16 + c]]

    @pl.loop(0, 24)
    def _(i):
        q, h, t = i // 8, (i // 4) % 2, i % 4
        pk = part[q]
        acc = jnp.zeros((256, 256), F32)
        rows = pl.ds(pl.multiple_of(t * 256, 256), 256)
        for cp in range(8):
            lhs = jnp.concatenate([ld[q, 2 * cp, rows, :], ld[q, 2 * cp + 1, rows, :]], axis=1)
            parts = []
            for c in (2 * cp, 2 * cp + 1):
                re = g[pk, h, 0, c * 64 : (c + 1) * 64, :]
                im = g[pk, h, 1, c * 64 : (c + 1) * 64, :]
                parts += [jnp.concatenate([re, im], axis=1), jnp.concatenate([-im, re], axis=1)]
            acc += jnp.dot(lhs, jnp.concatenate(parts, axis=0), preferred_element_type=F32)
        xs[q, h, rows, :] = acc.astype(BF16)

    @pl.loop(0, 16)
    def _(i):
        for u in range(4):
            e = i * 4 + u
            rr = pl.ds(pl.multiple_of(ex[0, e] * 64, 64), 64)
            ss = pl.ds(pl.multiple_of(ex[1, e] * 64, 64), 64)
            acc = jnp.zeros((64, 128), F32)
            for q in range(3):
                for h in range(2):
                    a, b = xs[q, h, rr, :], xs[q, h, ss, :]
                    w = jnp.concatenate([-b[:, 128:], b[:, :128]], axis=1)
                    acc += lax.dot_general(a, jnp.concatenate([b, w], axis=0), NT, preferred_element_type=F32)
            for p in range(2):
                piece = acc[p * 32 : (p + 1) * 32]
                sf[p, i // 4, i % 4, u] = piece
                sb[p, i // 4, i % 4, u] = piece.astype(BF16)


def local(idx, part, ex, lin, g):
    smem = pl.BlockSpec(memory_space=pltpu.SMEM)
    vmem = pl.BlockSpec(memory_space=pltpu.VMEM)
    shape = (2, 4, 4, 4, 32, 128)
    return pl.pallas_call(
        local_kernel,
        out_shape=(jax.ShapeDtypeStruct(shape, F32), jax.ShapeDtypeStruct(shape, BF16)),
        in_specs=[smem] * 3 + [vmem] * 2,
        out_specs=(vmem, vmem),
        scratch_shapes=[
            pltpu.VMEM((145, 64, 128), BF16),
            pltpu.VMEM((3, 16, 1024, 128), BF16),
            pltpu.VMEM((3, 2, 1024, 256), BF16),
        ],
        compiler_params=pltpu.CompilerParams(vmem_limit_bytes=56 * 2**20),
        name="local",
    )(idx, part, ex, lin, g)


def scatter_kernel(factor, sf, sb, out, ra, rb, t, a1f, a1b, qa, qb, qt, a2f, a2b, zin, ss, rs, zs, zr):
    zh, c, x, y, zl = place()

    def nb(dx, dy):
        return device(zh, c, (x + dx + 4) % 4, (y + dy + 4) % 4, zl)

    zdev = [device(zh, c, x, y, (zl + j) % 4) for j in range(1, 4)]
    ax = (nb(1, 0), nb(-1, 0))
    ay = (nb(0, 1), nb(0, -1))
    greet(zdev + list(ax) + list(ay))

    def begin(n, axis, blk, r1, r2):
        up, down = axis
        out = []
        out.append(rcopy(blk(2, 0), r1.at[0], ss.at[n, 0], rs.at[n, 0], up))
        out.append(rcopy(blk(2, 1), r1.at[1], ss.at[n, 1], rs.at[n, 1], down))
        out.append(rcopy(blk(1, 1), r2.at[0], ss.at[n, 2], rs.at[n, 2], up))
        out.append(rcopy(blk(-1, 0), r2.at[1], ss.at[n, 3], rs.at[n, 3], down))
        for cp in out:
            cp.start()
        return out

    def middle(n, axis, first, val, r1, tmp, r3):
        out = []
        for i in range(2):
            first[i].wait_recv()
            tmp[i] = (r1[i].astype(F32) + val((1, -1)[i], i)).astype(BF16)
            cp = rcopy(tmp.at[i], r3.at[i], ss.at[n, 4 + i], rs.at[n, 4 + i], axis[i])
            cp.start()
            out.append(cp)
        return out

    def blk1(p):
        def f(d, i):
            j = (((x if p == 0 else y) + d + 4) % 4)
            if p == 0:
                return sb.at[0, j, 2 * i : 2 * i + 2]
            return sb.at[1, 2 * i : 2 * i + 2, j]

        return f

    def val1(p):
        def f(d, i):
            j = (((x if p == 0 else y) + d + 4) % 4)
            if p == 0:
                return sf[0, j, 2 * i : 2 * i + 2]
            return sf[1, 2 * i : 2 * i + 2, j]

        return f

    axis1, axis2 = (ax, ay), (ay, ax)
    first = [begin(p, axis1[p], blk1(p), ra.at[p, 0], ra.at[p, 1]) for p in range(2)]
    mid = [middle(p, axis1[p], first[p], val1(p), ra.at[p, 0], t.at[p], rb.at[p]) for p in range(2)]
    first2 = []
    sent = first + mid

    def blk2(p):
        return lambda d, i: a1b.at[p, ((y if p == 0 else x) + d + 4) % 4, 2 * i : 2 * i + 2]

    def val2(p):
        return lambda d, i: a1f[p, ((y if p == 0 else x) + d + 4) % 4, 2 * i : 2 * i + 2]

    for p in range(2):
        first[p][2].wait_recv()
        first[p][3].wait_recv()
        for i in range(2):
            mid[p][i].wait_recv()
            v = val1(p)(0, i) + ra[p, 1, 1 - i].astype(F32) + rb[p, i].astype(F32)
            a1f[p, 2 * i : 2 * i + 2] = v
            a1b[p, 2 * i : 2 * i + 2] = v.astype(BF16)
        first2.append(begin(2 + p, axis2[p], blk2(p), qa.at[p, 0], qa.at[p, 1]))
    mid2 = [middle(2 + p, axis2[p], first2[p], val2(p), qa.at[p, 0], qt.at[p], qb.at[p]) for p in range(2)]
    for p in range(2):
        first2[p][2].wait_recv()
        first2[p][3].wait_recv()
        for i in range(2):
            mid2[p][i].wait_recv()
            v = val2(p)(0, i) + qa[p, 1, 1 - i].astype(F32) + qb[p, i].astype(F32)
            a2f[p, 2 * i : 2 * i + 2] = v
            a2b[p, 2 * i : 2 * i + 2] = v.astype(BF16)
    zc = []
    for j in range(3):
        cp = rcopy(a2b.at[:, (zl + j + 1) % 4], zin.at[j], zs.at[j], zr.at[j], zdev[j])
        cp.start()
        zc.append(cp)
    total = a2f[:, zl]
    for j in range(3):
        zc[j].wait_recv()
        total = total + zin[j].astype(F32)
    total = total * factor
    out[0:32] = total[0]
    out[32:64] = total[1]
    for cp in zc:
        cp.wait_send()
    for cps in sent + first2 + mid2:
        for cp in cps:
            cp.wait_send()


def scatter(factor, sf, sb):
    vmem = pl.BlockSpec(memory_space=pltpu.VMEM)
    dma = pltpu.SemaphoreType.DMA
    half, quarter = (2, 4, 32, 128), (2, 32, 128)

    def kern(*refs):
        scatter_kernel(factor, *refs)

    return pl.pallas_call(
        kern,
        out_shape=jax.ShapeDtypeStruct((64, 128), F32),
        in_specs=[vmem, vmem],
        out_specs=vmem,
        scratch_shapes=[
            pltpu.VMEM((2, 2, 2) + half, BF16),
            pltpu.VMEM((2, 2) + half, BF16),
            pltpu.VMEM((2, 2) + half, BF16),
            pltpu.VMEM((2, 4, 4, 32, 128), F32),
            pltpu.VMEM((2, 4, 4, 32, 128), BF16),
            pltpu.VMEM((2, 2, 2) + quarter, BF16),
            pltpu.VMEM((2, 2) + quarter, BF16),
            pltpu.VMEM((2, 2) + quarter, BF16),
            pltpu.VMEM((2, 4, 32, 128), F32),
            pltpu.VMEM((2, 4, 32, 128), BF16),
            pltpu.VMEM((3, 2, 32, 128), BF16),
            dma((4, 6)),
            dma((4, 6)),
            dma((3,)),
            dma((3,)),
        ],
        compiler_params=pltpu.CompilerParams(collective_id=1, has_side_effects=True),
        name="scatter",
    )(sf, sb)


def on_device(integrals, block_lists, coeff, match, ex_blocks):
    nq, naux, occ = 3, 64, 256
    factor = -((nq * naux * occ) ** (-0.5))
    lists = block_lists[:, 0, 0]
    cells = lists[:, 0] * 16 + lists[:, 1]
    number = jnp.arange(144, dtype=jnp.int32).reshape(3, 1, 48)
    hit = cells[:, None, :] == jnp.arange(256, dtype=jnp.int32)[None, :, None]
    idx = jnp.min(jnp.where(hit, number, 144), axis=2)
    part = lax.dynamic_index_in_dim(match, lax.axis_index("ka"), axis=1, keepdims=False)
    g = gather(coeff).reshape(4, 2, 2, 1024, 128)
    sf, sb = local(idx, part, ex_blocks[0], integrals.reshape(144, 64, 128), g)
    return scatter(factor, sf, sb)[None]


def solution(mesh):
    return jax.shard_map(
        on_device,
        mesh=mesh,
        in_specs=(
            P(None, "ka", "fit", None, None, None),
            P(None, "ka", "fit", None, None),
            P("ka", None, "fit", None),
            P(),
            P("ka", None, None),
        ),
        out_specs=P("ka", "fit", None),
        check_vma=False,
    )
```

time: 1860 us -> 94.9 us (0.05)
  waiting for transfers between devices: 1710 us -> 0 us
  Pallas kernels: 0 us -> 90.2 us
  matrix products: 42.1 us -> 0 us
  local copies, waits for them, and re-layouts: 44.9 us -> 2.83 us
  between operations: 19.3 us -> 0.02 us
    all_gather x3 -> x0, waiting for transfers between devices: 991 us -> none  [on_device(): lax.all_gather(jnp.take(shards, partner, axis=0), 'fit', axis=2, tiled=True)]
    psum x1 -> x0, waiting for transfers between devices: 721 us -> none  [on_device(): whole = lax.psum(pending, 'fit')]
    pallas_call x0 -> x3, Pallas kernels: none -> 90.2 us  [the longest x1 37.3 us: gather(): pl.pallas_call(gather_kernel, out_shape=jax.ShapeDtypeStruct(shape, BF16)...]
    dot_general x12 -> x0, matrix products: 42.1 us -> none  [the longest x3 17.2 us: half_transform(): jnp.einsum('rb,bmj->rmj', onehot, prods, precision=lax.Precision.HIGHEST)]
    gather x9 -> x0, local copies, waits for them, and re-layouts: 32.4 us -> none  [the longest x3 15.4 us: half_transform(): picked = jnp.take(operands, lists[1], axis=0)]
  transfers between devices with their start and end apart: 4 -> 0, of which waited for: 4 -> 0; matrix products, arithmetic and copies ran while one was open for 3% -> 0% of each run, Pallas kernels for 0% -> 0%
where the time goes in v1:
time: 94.9 us; the launch traced here: 94.5 us
  Pallas kernels  90.2 us (95%)
  local copies, waits for them, and re-layouts  2.83 us (3%)
  other arithmetic  1.49 us (2%)
    pallas_call x1, Pallas kernels, gather(): pl.pallas_call(gather_kernel, out_shape=jax.ShapeDtypeStruct(shape, BF16)...  37.3 us
    pallas_call x1, Pallas kernels, local(): pl.pallas_call(local_kernel, out_shape=(jax.ShapeDtypeStruct(shape, F32),...  28.9 us
    pallas_call x1, Pallas kernels, scatter(): pl.pallas_call(kern, out_shape=jax.ShapeDtypeStruct((64, 128), F32), in_s...  24 us
    unnamed x4, local copies, waits for them, and re-layouts  2.06 us

profile of v1, /device:TPU:8, one launch (start us, length us, event | category | flops | bytes accessed | tf_op | source)
XLA Modules:
  0.0 94.5 jit_solution(8901602793274274256)
XLA Ops:
  0.0 0.0 copy-start
  0.0 0.7 copy-done
  0.7 0.8 dynamic-slice_reduce_fusion.part
  1.5 0.8 slice_add_fusion
  2.2 0.7 select_reduce_fusion.idx
  3.0 37.3 %gather.1 = bf16[2,2,2,2,4,4,64,128]{7,6,5,4,3,2,1,0:T(8,128)(2,1)} custom-call(bf16[1,2,16,256]{3,2,1,0:T(8,128)(2,1)} %coeff.1), custom_call_target="tpu_custom_call" | custom-call | tf_op jit(solution)/shard_map/gather/pallas_call | solution.py:148
  40.2 28.9 %local.1 = (f32[2,4,4,4,32,128]{5,4,3,2,1,0:T(8,128)}, bf16[2,4,4,4,32,128]{5,4,3,2,1,0:T(8,128)(2,1)}) custom-call(s32[3,256]{1,0:T(4,128)} %select_reduce_fusion.idx, s32[3]{0:T(128)} %dynamic-slice_reduce_fusion.part, s32[2,64]{1,0:T(2,128)} %bitcast.13, bf16[144,64,128]{2,1,0:T(8,128)(2,1)} %bitcast.9, bf16[4,2,2,1024,128]{4,3,2,1,0:T(8,128)(2,1)} %bitcast.8), custom_call_target="tpu_custom_call" | custom-call | tf_op jit(solution)/shard_map/local/pallas_call | solution.py:216
  69.1 24.0 %scatter.1 = f32[64,128]{1,0:T(8,128)} custom-call(f32[2,4,4,4,32,128]{5,4,3,2,1,0:T(8,128)} %get-tuple-element.7.refs_0_, bf16[2,4,4,4,32,128]{5,4,3,2,1,0:T(8,128)(2,1)} %get-tuple-element.8.refs_1_), custom_call_target="tpu_custom_call" | custom-call | tf_op jit(solution)/shard_map/scatter/pallas_call | solution.py:338
  93.1 1.4 %copy.10 = f32[1,64,128]{2,1,0:T(8,128)} copy(f32[1,64,128]{2,1,0:T(8,128)} %bitcast.10) | data formatting | bytes 65536
  (2 shorter events, 0.0 us)
Async XLA Ops:
  0.0 0.7 copy-start

commit v2 on v0

v2 whole, which is shorter than its diff:
```python
import jax
import jax.numpy as jnp
from jax import lax
from jax.experimental import pallas as pl
from jax.experimental.pallas import tpu as pltpu
from jax.sharding import PartitionSpec as P

MESH = pl.DeviceIdType.MESH
NT = (((1,), (1,)), ((), ()))
F32 = jnp.float32
BF16 = jnp.bfloat16


def place():
    ka, fit = lax.axis_index("ka"), lax.axis_index("fit")
    x, y, zl = fit // 16, (fit // 4) % 4, fit % 4
    return ka // 2, ka % 2, x, y, zl


def device(zh, c, x, y, zl):
    return (zh * 2 + c, x * 16 + y * 4 + zl)


def rcopy(src, dst, ssem, rsem, dev):
    return pltpu.make_async_remote_copy(
        src_ref=src, dst_ref=dst, send_sem=ssem, recv_sem=rsem, device_id=dev, device_id_type=MESH
    )


def greet(devices):
    barrier = pltpu.get_barrier_semaphore()
    for dev in devices:
        pl.semaphore_signal(barrier, inc=1, device_id=dev, device_id_type=MESH)
    pl.semaphore_wait(barrier, len(devices))


def fused_kernel(factor, idx, match, ex, coeff, lin, out, *scratch):
    (ga, gb, ga_m, gb_m, ga_p, gb_p, ga_2, gb_2, lv, ld, xa, xs, sd, sf, sb, ra, rb, t, a1f, a1b, qa, qb, qt, a2f, a2b, zin, where) = scratch[:27]
    lsem, zs, zr, rs, rr, bs, br, ss, sr, ws, wr = scratch[27:]
    gs = ({0: ga, -1: ga_m, 1: ga_p, 2: ga_2}, {0: gb, -1: gb_m, 1: gb_p, 2: gb_2})
    zh, c, x, y, zl = place()
    z = zh * 4 + zl
    own = pl.ds(pl.multiple_of(zl * 16, 16), 16)
    loads = []
    for h in range(2):
        for s in range(2):
            cp = pltpu.make_async_copy(
                coeff.at[0, s, :, h * 128 : (h + 1) * 128],
                (ga.at[c * 2 + zh, s, y, own], gb.at[c * 2 + zh, s, x, own])[h],
                lsem.at[h * 2 + s],
            )
            cp.start()
            loads.append(cp)
    lcopy = pltpu.make_async_copy(lin, lv.at[0:144], lsem.at[4])
    lcopy.start()
    for k in range(4):
        where[k] = (k % 2) * 2 + k // 2

    def nb(dx, dy):
        return device(zh, c, (x + dx + 4) % 4, (y + dy + 4) % 4, zl)

    zdev = []
    for j in range(1, 8):
        zz = (z + j) % 8
        zdev.append(device(zz // 4, c, x, y, zz % 4))
    wdev = [device(zh, c, x, y, (zl + j) % 4) for j in range(1, 4)]
    sib = device(zh, 1 - c, x, y, zl)
    ax = (nb(1, 0), nb(-1, 0))
    ay = (nb(0, 1), nb(0, -1))
    greet(zdev + list(ax) + list(ay) + [sib])
    for cp in loads:
        cp.wait()

    mine = pl.ds(c * 2, 2)
    pieces = (ga.at[c * 2 + zh, :, y, own], gb.at[c * 2 + zh, :, x, own])
    zc = [rcopy(p, p, zs.at[j, h], zr.at[j, h], zdev[j]) for j in range(7) for h, p in enumerate(pieces)]
    for cp in zc:
        cp.start()

    lcopy.wait()
    lv[144] = jnp.zeros((64, 128), BF16)

    @pl.loop(0, 48)
    def _(i):
        q, cc = i // 16, i % 16
        for r in range(16):
            ld[q, cc, r * 64 : (r + 1) * 64, :] = lv[idx[q, r * 16 + cc]]

    for cp in zc:
        cp.wait()

    def ring(n, axis, src, dst):
        first = {}
        for s in range(2):
            for i in range(2):
                k = s if i == 0 else 1 - s
                cp = rcopy(src(k), dst[i](k), rs.at[n, i, k], rr.at[n, i, k], axis[i])
                cp.start()
                first[i, k] = cp
        return first

    def relay(n, axis, first, src, dst):
        cps = []
        for i in range(2):
            first[i, i].wait_recv()
            cp = rcopy(src[i](i), dst(i), rs.at[n, 2, i], rr.at[n, 2, i], axis[i])
            cp.start()
            cps.append(cp)
        return cps

    def row(h, d):
        return lambda k: gs[h][0].at[mine, k, ((y, x)[h] + d + 4) % 4]

    def whole(h, d):
        return lambda k: gs[h][d].at[mine, k]

    fa, fb = (ring(h, (ay, ax)[h], row(h, 0), [row(h, 0)] * 2) for h in range(2))
    ra2, rb2 = (
        relay(h, (ay, ax)[h], (fa, fb)[h], [row(h, -1), row(h, 1)], lambda k, h=h: row(h, (-1, 1)[k])(k))
        for h in range(2)
    )
    for f in (fa, fb):
        f[0, 1].wait_recv()
        f[1, 0].wait_recv()
    for cp in ra2 + rb2:
        cp.wait_recv()
    fa3, fb3 = (ring(2 + h, (ax, ay)[h], whole(h, 0), [whole(h, -1), whole(h, 1)]) for h in range(2))
    sibs = {}

    def to_sib(h, d):
        sibs[h, d] = []
        for k in range(2):
            ref = whole(h, d)(k)
            cp = rcopy(ref, ref, bs.at[h, d + 1, k], br.at[h, d + 1, k], sib)
            cp.start()
            sibs[h, d].append(cp)

    def from_sib(h, d):
        for cp in sibs[h, d]:
            cp.wait_recv()

    def chunk(h, d, first, last):
        j = ((x if h == 0 else y) + d + 4) % 4

        @pl.loop(0, 3)
        def _(q):
            pk = where[match[q, zh * 2 + c]]
            left, right = [], []
            for i in range(4):
                bx, by = (j, i) if h == 0 else (i, j)
                left.append(ld[q, bx * 4 + by])
                re, im = (gs[h][d][pk, s, i] for s in range(2))
                right += [jnp.concatenate([re, im], axis=1), jnp.concatenate([-im, re], axis=1)]
            v = jnp.dot(
                jnp.concatenate(left, axis=1), jnp.concatenate(right, axis=0), preferred_element_type=F32
            )
            if not first:
                v = v + xa[q, h]
            if last:
                xs[q, h] = v.astype(BF16)
            else:
                xa[q, h] = v

    to_sib(0, 0)
    to_sib(1, 0)
    for h in range(2):
        from_sib(h, 0)
        chunk(h, 0, True, False)
    ra3, rb3 = (
        relay(2 + h, (ax, ay)[h], (fa3, fb3)[h], [whole(h, -1), whole(h, 1)], whole(h, 2)) for h in range(2)
    )
    for f in (fa3, fb3):
        f[0, 1].wait_recv()
        f[1, 0].wait_recv()
    for d in (-1, 1):
        to_sib(0, d)
        to_sib(1, d)
    for h in range(2):
        from_sib(h, -1)
        chunk(h, -1, False, False)
    for cp in ra3 + rb3:
        cp.wait_recv()
    to_sib(0, 2)
    to_sib(1, 2)
    for h in range(2):
        from_sib(h, 1)
        chunk(h, 1, False, False)
    for h in range(2):
        from_sib(h, 2)
        chunk(h, 2, False, True)

    @pl.loop(0, 8)
    def _(i):
        cols = pl.ds(pl.multiple_of(i * 128, 128), 128)
        left, right = [], []
        for q in range(3):
            for h in range(2):
                b = xs[q, h, cols, :]
                w = jnp.concatenate([-b[:, 128:], b[:, :128]], axis=1)
                left.append(xs[q, h])
                right.append(jnp.concatenate([b[:64], w[:64], b[64:], w[64:]], axis=0))
        acc = lax.dot_general(left[0], right[0], NT, preferred_element_type=F32)
        for k in range(1, 6):
            acc += lax.dot_general(left[k], right[k], NT, preferred_element_type=F32)
        sd[2 * i] = acc[:, :128].reshape(16, 64, 128)
        sd[2 * i + 1] = acc[:, 128:].reshape(16, 64, 128)

    @pl.loop(0, 16)
    def _(i):
        for u in range(4):
            e = i * 4 + u
            v = sd[ex[1, e], ex[0, e]]
            for p in range(2):
                half = v[p * 32 : (p + 1) * 32]
                sf[p, i // 4, i % 4, u] = half
                sb[p, i // 4, i % 4, u] = half.astype(BF16)

    def begin(n, axis, blk, r1, r2):
        up, down = axis
        cps = [
            rcopy(blk(2, 0), r1.at[0], ss.at[n, 0], sr.at[n, 0], up),
            rcopy(blk(2, 1), r1.at[1], ss.at[n, 1], sr.at[n, 1], down),
            rcopy(blk(1, 1), r2.at[0], ss.at[n, 2], sr.at[n, 2], up),
            rcopy(blk(-1, 0), r2.at[1], ss.at[n, 3], sr.at[n, 3], down),
        ]
        for cp in cps:
            cp.start()
        return cps

    def middle(n, axis, first, val, r1, tmp, r3):
        cps = []
        for i in range(2):
            first[i].wait_recv()
            tmp[i] = (r1[i].astype(F32) + val((1, -1)[i], i)).astype(BF16)
            cp = rcopy(tmp.at[i], r3.at[i], ss.at[n, 4 + i], sr.at[n, 4 + i], axis[i])
            cp.start()
            cps.append(cp)
        return cps

    def pick1(ref, p):
        def f(d, i):
            j = ((x if p == 0 else y) + d + 4) % 4
            return ref.at[0, j, 2 * i : 2 * i + 2] if p == 0 else ref.at[1, 2 * i : 2 * i + 2, j]

        return f

    def pick2(ref, p):
        return lambda d, i: ref.at[p, ((y if p == 0 else x) + d + 4) % 4, 2 * i : 2 * i + 2]

    def stage(n, axes, fblk, bblk, r1, r2, r3, tmp):
        first = [begin(n + p, axes[p], bblk[p], r1.at[p], r2.at[p]) for p in range(2)]
        val = [lambda d, i, p=p: fblk[p](d, i)[...] for p in range(2)]
        mid = [middle(n + p, axes[p], first[p], val[p], r1.at[p], tmp.at[p], r3.at[p]) for p in range(2)]
        return first, mid, val

    def finish(first, mid, val, r2, r3, p, i):
        first[p][3 - i].wait_recv()
        mid[p][i].wait_recv()
        return val[p](0, i) + r2[p, 1 - i].astype(F32) + r3[p, i].astype(F32)

    f1, m1, v1 = stage(
        0, (ax, ay), [pick1(sf, p) for p in range(2)], [pick1(sb, p) for p in range(2)], ra.at[0], ra.at[1], rb, t
    )
    for p in range(2):
        for i in range(2):
            v = finish(f1, m1, v1, ra.at[1], rb, p, i)
            a1f[p, 2 * i : 2 * i + 2] = v
            a1b[p, 2 * i : 2 * i + 2] = v.astype(BF16)
    f2, m2, v2 = stage(
        2, (ay, ax), [pick2(a1f, p) for p in range(2)], [pick2(a1b, p) for p in range(2)], qa.at[0], qa.at[1], qb, qt
    )
    for p in range(2):
        for i in range(2):
            v = finish(f2, m2, v2, qa.at[1], qb, p, i)
            a2f[p, 2 * i : 2 * i + 2] = v
            a2b[p, 2 * i : 2 * i + 2] = v.astype(BF16)
    wc = []
    for j in range(3):
        cp = rcopy(a2b.at[:, (zl + j + 1) % 4], zin.at[j], ws.at[j], wr.at[j], wdev[j])
        cp.start()
        wc.append(cp)
    total = a2f[:, zl]
    for j in range(3):
        wc[j].wait_recv()
        total = total + zin[j].astype(F32)
    total = total * factor
    out[0:32] = total[0]
    out[32:64] = total[1]
    for f in (fa, fb, fa3, fb3):
        for cp in f.values():
            cp.wait_send()
    for cps in sibs.values():
        for cp in cps:
            cp.wait_send()
    for cps in [ra2, rb2, ra3, rb3, wc] + f1 + m1 + f2 + m2:
        for cp in cps:
            cp.wait_send()


def fused(factor, idx, match, ex, coeff, lin):
    smem = pl.BlockSpec(memory_space=pltpu.SMEM)
    vmem = pl.BlockSpec(memory_space=pltpu.VMEM)
    hbm = pl.BlockSpec(memory_space=pl.ANY)
    dma = pltpu.SemaphoreType.DMA
    half, quarter = (2, 4, 32, 128), (2, 32, 128)
    blocks = (2, 4, 4, 4, 32, 128)

    def kern(*refs):
        fused_kernel(factor, *refs)

    return pl.pallas_call(
        kern,
        out_shape=jax.ShapeDtypeStruct((64, 128), F32),
        in_specs=[smem] * 3 + [hbm] * 2,
        out_specs=vmem,
        scratch_shapes=[pltpu.VMEM((4, 2, 4, 64, 128), BF16)] * 8
        + [
            pltpu.VMEM((145, 64, 128), BF16),
            pltpu.VMEM((3, 16, 1024, 128), BF16),
            pltpu.VMEM((3, 2, 1024, 256), F32),
            pltpu.VMEM((3, 2, 1024, 256), BF16),
            pltpu.VMEM((16, 16, 64, 128), F32),
            pltpu.VMEM(blocks, F32),
            pltpu.VMEM(blocks, BF16),
            pltpu.VMEM((2, 2, 2) + half, BF16),
            pltpu.VMEM((2, 2) + half, BF16),
            pltpu.VMEM((2, 2) + half, BF16),
            pltpu.VMEM((2, 4, 4, 32, 128), F32),
            pltpu.VMEM((2, 4, 4, 32, 128), BF16),
            pltpu.VMEM((2, 2, 2) + quarter, BF16),
            pltpu.VMEM((2, 2) + quarter, BF16),
            pltpu.VMEM((2, 2) + quarter, BF16),
            pltpu.VMEM((2, 4, 32, 128), F32),
            pltpu.VMEM((2, 4, 32, 128), BF16),
            pltpu.VMEM((3, 2, 32, 128), BF16),
            pltpu.SMEM((4,), jnp.int32),
            dma((5,)),
            dma((7, 2)),
            dma((7, 2)),
            dma((4, 3, 2)),
            dma((4, 3, 2)),
            dma((2, 4, 2)),
            dma((2, 4, 2)),
            dma((4, 6)),
            dma((4, 6)),
            dma((3,)),
            dma((3,)),
        ],
        compiler_params=pltpu.CompilerParams(
            collective_id=0, has_side_effects=True, vmem_limit_bytes=60 * 2**20
        ),
        name="fused",
    )(idx, match, ex, coeff, lin)


def on_device(integrals, block_lists, coeff, match, ex_blocks):
    nq, naux, occ = 3, 64, 256
    factor = -((nq * naux * occ) ** (-0.5))
    lists = block_lists[:, 0, 0]
    cells = lists[:, 0] * 16 + lists[:, 1]
    number = jnp.arange(144, dtype=jnp.int32).reshape(3, 1, 48)
    hit = cells[:, None, :] == jnp.arange(256, dtype=jnp.int32)[None, :, None]
    idx = jnp.min(jnp.where(hit, number, 144), axis=2)
    lin = integrals.reshape(144, 64, 128)
    return fused(factor, idx, match, ex_blocks[0], coeff, lin)[None]


def solution(mesh):
    return jax.shard_map(
        on_device,
        mesh=mesh,
        in_specs=(
            P(None, "ka", "fit", None, None, None),
            P(None, "ka", "fit", None, None),
            P("ka", None, "fit", None),
            P(),
            P("ka", None, None),
        ),
        out_specs=P("ka", "fit", None),
        check_vma=False,
    )
```

time: 1860 us -> 69.7 us (0.04)
  waiting for transfers between devices: 1710 us -> 0 us
  Pallas kernels: 0 us -> 66.6 us
  local copies, waits for them, and re-layouts: 44.9 us -> 1.38 us
  matrix products: 42.1 us -> 0 us
  between operations: 19.3 us -> 0.01 us
    all_gather x3 -> x0, waiting for transfers between devices: 991 us -> none  [on_device(): lax.all_gather(jnp.take(shards, partner, axis=0), 'fit', axis=2, tiled=True)]
    psum x1 -> x0, waiting for transfers between devices: 721 us -> none  [on_device(): whole = lax.psum(pending, 'fit')]
    pallas_call x0 -> x1, Pallas kernels: none -> 66.6 us  [fused(): pl.pallas_call(kern, out_shape=jax.ShapeDtypeStruct((64, 128), F32), in_s...]
    dot_general x12 -> x0, matrix products: 42.1 us -> none  [the longest x3 17.2 us: half_transform(): jnp.einsum('rb,bmj->rmj', onehot, prods, precision=lax.Precision.HIGHEST)]
    gather x9 -> x0, local copies, waits for them, and re-layouts: 32.4 us -> none  [the longest x3 15.4 us: half_transform(): picked = jnp.take(operands, lists[1], axis=0)]
  transfers between devices with their start and end apart: 4 -> 0, of which waited for: 4 -> 0; matrix products, arithmetic and copies ran while one was open for 3% -> 0% of each run, Pallas kernels for 0% -> 0%
where the time goes in v2:
time: 69.7 us; the launch traced here: 69.5 us
  Pallas kernels  66.6 us (96%)
  other arithmetic  1.49 us (2%)
  local copies, waits for them, and re-layouts  1.38 us (2%)
    pallas_call x1, Pallas kernels, fused(): pl.pallas_call(kern, out_shape=jax.ShapeDtypeStruct((64, 128), F32), in_s...  66.6 us

profile of v2, /device:TPU:8, one launch (start us, length us, event | category | flops | bytes accessed | tf_op | source)
XLA Modules:
  0.0 69.5 jit_solution(3102733040771893668)
XLA Ops:
  0.0 0.8 %slice_add_fusion = s32[3,1,48]{2,1,0:T(1,128)S(1)} fusion(s32[3,2,48]{2,1,0:T(2,128)} %bitcast.10), kind=kLoop, calls=%fused_computation.4 | loop fusion | flops 288 | bytes 1728 | tf_op jit(solution)/shard_map/add | solution.py:360
  0.8 0.7 %select_reduce_fusion.refs_0_ = s32[3,256]{1,0:T(4,128)} fusion(s32[3,48]{1,0:T(4,128)S(1)} %multiply_add_fusion, s32[3,48]{1,0:T(4,128)S(1)} %bitcast.9), kind=kLoop, calls=%fused_computation | loop fusion | flops 109824 | bytes 4224 | tf_op jit(solution)/shard_map/reduce_min | solution.py:363
  1.5 66.6 %fused.1 = f32[64,128]{1,0:T(8,128)} custom-call(s32[3,256]{1,0:T(4,128)} %select_reduce_fusion.refs_0_, s32[3,4]{1,0:T(4,128)} %refs_1_.1, s32[2,64]{1,0:T(2,128)} %bitcast.11, bf16[1,2,16,256]{3,2,1,0:T(8,128)(2,1)} %refs_3_.1, bf16[144,64,128]{2,1,0:T(8,128)(2,1)} %bitcast.7), custom_call_target="tpu_custom_call" | custom-call | tf_op jit(solution)/shard_map/fused/pallas_call | solution.py:311
  68.1 1.4 %copy.10 = f32[1,64,128]{2,1,0:T(8,128)} copy(f32[1,64,128]{2,1,0:T(8,128)} %bitcast.8) | data formatting | bytes 65536
  (2 shorter events, 0.0 us)

commit v3 on v2

v3 whole, which is shorter than its diff:
```python
import jax
import jax.numpy as jnp
from jax import lax
from jax.experimental import pallas as pl
from jax.experimental.pallas import tpu as pltpu
from jax.sharding import PartitionSpec as P

MESH = pl.DeviceIdType.MESH
NT = (((1,), (1,)), ((), ()))
F32 = jnp.float32
BF16 = jnp.bfloat16


def place():
    ka, fit = lax.axis_index("ka"), lax.axis_index("fit")
    x, y, zl = fit // 16, (fit // 4) % 4, fit % 4
    return ka // 2, ka % 2, x, y, zl


def device(zh, c, x, y, zl):
    return (zh * 2 + c, x * 16 + y * 4 + zl)


def rcopy(src, dst, ssem, rsem, dev):
    return pltpu.make_async_remote_copy(
        src_ref=src, dst_ref=dst, send_sem=ssem, recv_sem=rsem, device_id=dev, device_id_type=MESH
    )


def greet(devices):
    barrier = pltpu.get_barrier_semaphore()
    for dev in devices:
        pl.semaphore_signal(barrier, inc=1, device_id=dev, device_id_type=MESH)
    pl.semaphore_wait(barrier, len(devices))


def fused_kernel(factor, match, ex, lists, coeff, lin, out, *scratch):
    (ga, gb, ga_m, gb_m, ga_p, gb_p, ga_2, gb_2, lv, ld, xa, xs, sf, sb, rin, acc, zb, zin, table, where, idx) = scratch[:21]
    lsem, zs, zr, ps, pr, rs, rr, bs, br, ss, sr, ws, wr = scratch[21:]
    gs = ({0: ga, -1: ga_m, 1: ga_p, 2: ga_2}, {0: gb, -1: gb_m, 1: gb_p, 2: gb_2})
    zh, c, x, y, zl = place()
    z = zh * 4 + zl
    own = pl.ds(pl.multiple_of(zl * 16, 16), 16)
    loads = []
    for h in range(2):
        for s in range(2):
            cp = pltpu.make_async_copy(
                coeff.at[0, s, :, h * 128 : (h + 1) * 128],
                (ga.at[c * 2 + zh, s, y, own], gb.at[c * 2 + zh, s, x, own])[h],
                lsem.at[h * 2 + s],
            )
            cp.start()
            loads.append(cp)
    lcopy = pltpu.make_async_copy(lin, lv.at[0:144], lsem.at[4])
    lcopy.start()
    same = lax.broadcasted_iota(jnp.int32, (48, 48), 0) == lax.broadcasted_iota(jnp.int32, (48, 48), 1)
    for q in range(3):
        cells = lists[q, 0:1, :] * 16 + lists[q, 1:2, :]
        cells = jnp.sum(jnp.where(same, jnp.broadcast_to(cells, (48, 48)), 0), axis=1, keepdims=True)
        hit = jnp.broadcast_to(cells, (48, 256)) == lax.broadcasted_iota(jnp.int32, (48, 256), 1)
        number = lax.broadcasted_iota(jnp.int32, (48, 256), 0) + (q * 48 - 144)
        found = jnp.sum(jnp.where(hit, number, 0), axis=0, keepdims=True) + 144
        table[q : q + 1, :] = jnp.maximum(found, 0)
    tcopy = pltpu.make_async_copy(table, idx, lsem.at[5])
    tcopy.start()
    for k in range(4):
        where[k] = (k % 2) * 2 + k // 2

    def nb(dx, dy):
        return device(zh, c, (x + dx + 4) % 4, (y + dy + 4) % 4, zl)

    zdev = []
    for j in range(1, 8):
        zz = (z + j) % 8
        zdev.append(device(zz // 4, c, x, y, zz % 4))
    wdev = [device(zh, c, x, y, (zl + j) % 4) for j in range(1, 4)]
    sib = device(zh, 1 - c, x, y, zl)
    ax = (nb(1, 0), nb(-1, 0))
    ay = (nb(0, 1), nb(0, -1))
    plane = [nb(dx, dy) for dx in range(4) for dy in range(4) if dx or dy]
    greet(zdev + plane + [sib])
    for cp in loads:
        cp.wait()

    mine = pl.ds(c * 2, 2)
    pieces = (ga.at[c * 2 + zh, :, y, own], gb.at[c * 2 + zh, :, x, own])
    zc = [rcopy(p, p, zs.at[j, h], zr.at[j, h], zdev[j]) for j in range(7) for h, p in enumerate(pieces)]
    for cp in zc:
        cp.start()

    lcopy.wait()
    tcopy.wait()
    lv[144] = jnp.zeros((64, 128), BF16)

    @pl.loop(0, 48)
    def _(i):
        q, cc = i // 16, i % 16
        for r in range(16):
            ld[q, cc, r * 64 : (r + 1) * 64, :] = lv[idx[q, r * 16 + cc]]

    for cp in zc:
        cp.wait()

    def ring(n, axis, src, dst):
        first = {}
        for s in range(2):
            for i in range(2):
                k = s if i == 0 else 1 - s
                cp = rcopy(src(k), dst[i](k), rs.at[n, i, k], rr.at[n, i, k], axis[i])
                cp.start()
                first[i, k] = cp
        return first

    def relay(n, axis, first, src, dst):
        cps = []
        for i in range(2):
            first[i, i].wait_recv()
            cp = rcopy(src[i](i), dst(i), rs.at[n, 2, i], rr.at[n, 2, i], axis[i])
            cp.start()
            cps.append(cp)
        return cps

    def whole(h, d):
        return lambda k: gs[h][d].at[mine, k]

    pc = []
    for d in range(1, 4):
        for h in range(2):
            ref = gs[h][0].at[mine, :, (y, x)[h]]
            cp = rcopy(ref, ref, ps.at[h, d - 1], pr.at[h, d - 1], (nb(0, d), nb(d, 0))[h])
            cp.start()
            pc.append(cp)
    for cp in pc:
        cp.wait_recv()
    fa3, fb3 = (ring(h, (ax, ay)[h], whole(h, 0), [whole(h, -1), whole(h, 1)]) for h in range(2))
    sibs = {}

    def to_sib(h, d):
        sibs[h, d] = []
        for k in range(2):
            ref = whole(h, d)(k)
            cp = rcopy(ref, ref, bs.at[h, d + 1, k], br.at[h, d + 1, k], sib)
            cp.start()
            sibs[h, d].append(cp)

    def from_sib(h, d):
        for cp in sibs[h, d]:
            cp.wait_recv()

    def chunk(h, d, first, last):
        j = ((x if h == 0 else y) + d + 4) % 4

        @pl.loop(0, 3)
        def _(q):
            pk = where[match[q, zh * 2 + c]]
            left, right = [], []
            for i in range(4):
                bx, by = (j, i) if h == 0 else (i, j)
                left.append(ld[q, bx * 4 + by])
                re, im = (gs[h][d][pk, s, i] for s in range(2))
                right += [jnp.concatenate([re, im], axis=1), jnp.concatenate([-im, re], axis=1)]
            v = jnp.dot(
                jnp.concatenate(left, axis=1), jnp.concatenate(right, axis=0), preferred_element_type=F32
            )
            if not first:
                v = v + xa[q, h]
            if last:
                xs[q, h] = v.astype(BF16).reshape(16, 64, 256)
            else:
                xa[q, h] = v

    to_sib(0, 0)
    to_sib(1, 0)
    for h in range(2):
        from_sib(h, 0)
        chunk(h, 0, True, False)
    ra3, rb3 = (
        relay(h, (ax, ay)[h], (fa3, fb3)[h], [whole(h, -1), whole(h, 1)], whole(h, 2)) for h in range(2)
    )
    for f in (fa3, fb3):
        f[0, 1].wait_recv()
        f[1, 0].wait_recv()
    for d in (-1, 1):
        to_sib(0, d)
        to_sib(1, d)
    for h in range(2):
        from_sib(h, -1)
        chunk(h, -1, False, False)
    for cp in ra3 + rb3:
        cp.wait_recv()
    to_sib(0, 2)
    to_sib(1, 2)
    for h in range(2):
        from_sib(h, 1)
        chunk(h, 1, False, False)
    for h in range(2):
        from_sib(h, 2)
        chunk(h, 2, False, True)

    def column(dx, dy):
        return (x + dx) % 4, (y + dy) % 4

    def send(i, jj):
        cx, cy = column((i + 1) % 4, (i + 1 + jj) % 4)
        slot = jj * 4 + i
        return rcopy(sb.at[slot], rin.at[slot], ss.at[slot], sr.at[slot], device(zh, c, cx, cy, zl))

    @pl.loop(0, 4)
    def _(jj):
        for i in range(4):
            cx, cy = column((i + 1) % 4, (i + 1 + jj) % 4)
            for u in range(4):
                e = (cx * 4 + cy) * 4 + u
                r, s = ex[0, e], ex[1, e]
                left, right = [], []
                for q in range(3):
                    for h in range(2):
                        a = xs[q, h, r]
                        left.append(
                            jnp.concatenate([a, jnp.concatenate([a[:, 128:], -a[:, :128]], axis=1)], axis=0)
                        )
                        right.append(xs[q, h, s])
                v = lax.dot_general(
                    jnp.concatenate(left, axis=1), jnp.concatenate(right, axis=1), NT, preferred_element_type=F32
                )
                v = jnp.concatenate([v[:64], v[64:]], axis=1)
                sb[jj * 4 + i, u] = v.astype(BF16)
                if i == 3:
                    sf[jj, u] = v
            if i < 3:
                send(i, jj).start()
            else:

                @pl.when(jj > 0)
                def _():
                    send(3, jj).start()

    acc[...] = sf[0]
    sent = []
    for jj in range(4):
        for i in range(4):
            if i == 3 and jj == 0:
                continue
            cp = send(i, jj)
            sent.append(cp)
            cp.wait_recv()
            acc[...] += rin[jj * 4 + i].astype(F32)
    zb[...] = acc[...].astype(BF16)
    wc = []
    for j in range(3):
        cp = rcopy(zb.at[(zl + j + 1) % 4], zin.at[j], ws.at[j], wr.at[j], wdev[j])
        cp.start()
        wc.append(cp)
    total = acc[zl]
    for j in range(3):
        wc[j].wait_recv()
        total = total + zin[j].astype(F32)
    out[...] = total * factor
    for f in (fa3, fb3):
        for cp in f.values():
            cp.wait_send()
    for cps in sibs.values():
        for cp in cps:
            cp.wait_send()
    for cp in pc + ra3 + rb3 + sent + wc:
        cp.wait_send()


def fused(factor, match, ex, lists, coeff, lin):
    smem = pl.BlockSpec(memory_space=pltpu.SMEM)
    vmem = pl.BlockSpec(memory_space=pltpu.VMEM)
    hbm = pl.BlockSpec(memory_space=pl.ANY)
    dma = pltpu.SemaphoreType.DMA

    def kern(*refs):
        fused_kernel(factor, *refs)

    return pl.pallas_call(
        kern,
        out_shape=jax.ShapeDtypeStruct((64, 128), F32),
        in_specs=[smem] * 2 + [vmem] + [hbm] * 2,
        out_specs=vmem,
        scratch_shapes=[pltpu.VMEM((4, 2, 4, 64, 128), BF16)] * 8
        + [
            pltpu.VMEM((145, 64, 128), BF16),
            pltpu.VMEM((3, 16, 1024, 128), BF16),
            pltpu.VMEM((3, 2, 1024, 256), F32),
            pltpu.VMEM((3, 2, 16, 64, 256), BF16),
            pltpu.VMEM((4, 4, 64, 128), F32),
            pltpu.VMEM((16, 4, 64, 128), BF16),
            pltpu.VMEM((16, 4, 64, 128), BF16),
            pltpu.VMEM((4, 64, 128), F32),
            pltpu.VMEM((4, 64, 128), BF16),
            pltpu.VMEM((3, 64, 128), BF16),
            pltpu.VMEM((3, 256), jnp.int32),
            pltpu.SMEM((4,), jnp.int32),
            pltpu.SMEM((3, 256), jnp.int32),
            dma((6,)),
            dma((7, 2)),
            dma((7, 2)),
            dma((2, 3)),
            dma((2, 3)),
            dma((2, 3, 2)),
            dma((2, 3, 2)),
            dma((2, 4, 2)),
            dma((2, 4, 2)),
            dma((16,)),
            dma((16,)),
            dma((3,)),
            dma((3,)),
        ],
        compiler_params=pltpu.CompilerParams(
            collective_id=0, has_side_effects=True, vmem_limit_bytes=60 * 2**20
        ),
        name="fused",
    )(match, ex, lists, coeff, lin)


def on_device(integrals, block_lists, coeff, match, ex_blocks):
    nq, naux, occ = 3, 64, 256
    factor = -((nq * naux * occ) ** (-0.5))
    lin = integrals.reshape(144, 64, 128)
    return fused(factor, match, ex_blocks[0], block_lists[:, 0, 0], coeff, lin)[None]


def solution(mesh):
    return jax.shard_map(
        on_device,
        mesh=mesh,
        in_specs=(
            P(None, "ka", "fit", None, None, None),
            P(None, "ka", "fit", None, None),
            P("ka", None, "fit", None),
            P(),
            P("ka", None, None),
        ),
        out_specs=P("ka", "fit", None),
        check_vma=False,
    )
```

time: 69.7 us -> 61 us (0.88)
  the two profiles are of different devices: /device:TPU:8 before, /device:TPU:1 now
where the time goes in v3:
time: 61 us; the launch traced here: 60.8 us
  Pallas kernels  59.4 us (97%)
  local copies, waits for them, and re-layouts  1.38 us (2%)
    pallas_call x1, Pallas kernels, fused(): pl.pallas_call(kern, out_shape=jax.ShapeDtypeStruct((64, 128), F32), in_s...  59.4 us
    unnamed x1, local copies, waits for them, and re-layouts  1.38 us

profile of v3, /device:TPU:1, one launch (start us, length us, event | category | flops | bytes accessed | tf_op | source)
XLA Modules:
  0.0 60.8 jit_solution(339283314316834405)
XLA Ops:
  0.0 59.4 %fused.1 = f32[64,128]{1,0:T(8,128)} custom-call(s32[3,4]{1,0:T(4,128)} %refs_0_.1, s32[2,64]{1,0:T(2,128)} %bitcast.7, s32[3,2,48]{2,1,0:T(2,128)} %bitcast.6, bf16[1,2,16,256]{3,2,1,0:T(8,128)(2,1)} %refs_3_.1, bf16[144,64,128]{2,1,0:T(8,128)(2,1)} %bitcast.4), custom_call_target="tpu_custom_call" | custom-call | tf_op jit(solution)/shard_map/fused/pallas_call | solution.py:278
  59.4 1.4 %copy.7 = f32[1,64,128]{2,1,0:T(8,128)} copy(f32[1,64,128]{2,1,0:T(8,128)} %bitcast.5) | data formatting | bytes 65536

commit v4 on v0

v4 whole, which is shorter than its diff:
```python
import jax
import jax.numpy as jnp
from jax import lax
from jax.experimental import pallas as pl
from jax.experimental.pallas import tpu as pltpu
from jax.sharding import PartitionSpec as P

MESH = pl.DeviceIdType.MESH
NT = (((1,), (1,)), ((), ()))
F32 = jnp.float32
BF16 = jnp.bfloat16


def place():
    ka, fit = lax.axis_index("ka"), lax.axis_index("fit")
    x, y, zl = fit // 16, (fit // 4) % 4, fit % 4
    return ka // 2, ka % 2, x, y, zl


def device(zh, c, x, y, zl):
    return (zh * 2 + c, x * 16 + y * 4 + zl)


def rcopy(src, dst, ssem, rsem, dev):
    return pltpu.make_async_remote_copy(
        src_ref=src, dst_ref=dst, send_sem=ssem, recv_sem=rsem, device_id=dev, device_id_type=MESH
    )


def greet(devices):
    barrier = pltpu.get_barrier_semaphore()
    for dev in devices:
        pl.semaphore_signal(barrier, inc=1, device_id=dev, device_id_type=MESH)
    pl.semaphore_wait(barrier, len(devices))


def fused_kernel(factor, match, ex, lists, coeff, lin, out, *scratch):
    own, far = scratch[0:2], scratch[2:14]
    (lv, ld, xa, xs, sf, sb, rin, af, ab, qin, cf, cb, zin, table, where, idx) = scratch[14:30]
    lsem, zs, zr, ps, pr, rs, rr, bs, br, ss, sr, qs, qr, ws, wr = scratch[30:]
    zh, c, x, y, zl = place()
    z = zh * 4 + zl
    cell = (y, x)
    mine = pl.ds(c * 2, 2)
    dist = {-1: 0, 1: 1, 2: 2}
    loads = []
    for h in range(2):
        for s in range(2):
            cp = pltpu.make_async_copy(
                coeff.at[0, s, :, h * 128 : (h + 1) * 128],
                own[h].at[c * 2 + zh, cell[h], zl, s],
                lsem.at[h * 2 + s],
            )
            cp.start()
            loads.append(cp)
    lcopy = pltpu.make_async_copy(lin, lv.at[0:144], lsem.at[4])
    lcopy.start()

    def nb(dx, dy):
        return device(zh, c, (x + dx + 4) % 4, (y + dy + 4) % 4, zl)

    def cross(h, d):
        return (nb(0, d), nb(d, 0))[h]

    def along(h, d):
        return (nb(d, 0), nb(0, d))[h]

    zdev = []
    for j in range(1, 8):
        zz = (z + j) % 8
        zdev.append(device(zz // 4, c, x, y, zz % 4))
    wdev = [device(zh, c, x, y, (zl + j) % 4) for j in range(1, 4)]
    sib = device(zh, 1 - c, x, y, zl)
    greet(zdev + [f(0, d) for f in (cross, along) for d in range(1, 4)] + [sib])
    for cp in loads:
        cp.wait()

    zc = []
    for j in range(7):
        for h in range(2):
            ref = own[h].at[c * 2 + zh, cell[h], zl]
            cp = rcopy(ref, ref, zs.at[j, h], zr.at[j, h], zdev[j])
            cp.start()
            zc.append(cp)

    same = lax.broadcasted_iota(jnp.int32, (48, 48), 0) == lax.broadcasted_iota(jnp.int32, (48, 48), 1)
    for q in range(3):
        cells = lists[q, 0:1, :] * 16 + lists[q, 1:2, :]
        cells = jnp.sum(jnp.where(same, jnp.broadcast_to(cells, (48, 48)), 0), axis=1, keepdims=True)
        hit = jnp.broadcast_to(cells, (48, 256)) == lax.broadcasted_iota(jnp.int32, (48, 256), 1)
        number = lax.broadcasted_iota(jnp.int32, (48, 256), 0) + (q * 48 - 144)
        found = jnp.sum(jnp.where(hit, number, 0), axis=0, keepdims=True) + 144
        table[q : q + 1, :] = jnp.maximum(found, 0)
    tcopy = pltpu.make_async_copy(table, idx, lsem.at[5])
    tcopy.start()
    for k in range(4):
        where[k] = (k % 2) * 2 + k // 2
    lcopy.wait()
    lv[144] = jnp.zeros((64, 128), BF16)
    tcopy.wait()

    @pl.loop(0, 48)
    def _(i):
        q, cc = i // 16, i % 16
        for r in range(16):
            ld[q, cc, r * 64 : (r + 1) * 64, :] = lv[idx[q, r * 16 + cc]]

    for cp in zc:
        cp.wait()

    pc = []
    for d in range(1, 4):
        for h in range(2):
            ref = own[h].at[mine, cell[h]]
            cp = rcopy(ref, ref, ps.at[h, d - 1], pr.at[h, d - 1], cross(h, d))
            cp.start()
            pc.append(cp)
    for cp in pc:
        cp.wait_recv()

    def buf(h, d, k):
        return far[(h * 3 + dist[d]) * 2 + k]

    first, sibs, relays = {}, {}, []
    for s in range(2):
        for h in range(2):
            for i, d in enumerate((1, -1)):
                k = s if i == 0 else 1 - s
                cp = rcopy(
                    own[h].at[mine, 2 * k : 2 * k + 2],
                    buf(h, -d, k).at[mine],
                    rs.at[h, i, k],
                    rr.at[h, i, k],
                    along(h, d),
                )
                cp.start()
                first[h, i, k] = cp

    def to_sib(h, ref, n):
        cp = rcopy(ref.at[mine], ref.at[mine], bs.at[h, n], br.at[h, n], sib)
        cp.start()
        sibs[h, n] = cp

    def to_sib_far(h, d, k):
        to_sib(h, buf(h, d, k), 1 + dist[d] * 2 + k)

    def chunk(h, parts, begin, end):
        @pl.loop(0, 3)
        def _(q):
            pk = where[match[q, zh * 2 + c]]
            left, right = [], []
            for ref, n, i, d in parts:
                j = ((x, y)[h] + d + 4) % 4
                left.append(ld[q, j * 4 + i] if h == 0 else ld[q, i * 4 + j])
                re, im = (ref[pk, n, :, s].reshape(64, 128) for s in range(2))
                right += [jnp.concatenate([re, im], axis=1), jnp.concatenate([-im, re], axis=1)]
            v = jnp.dot(
                jnp.concatenate(left, axis=1), jnp.concatenate(right, axis=0), preferred_element_type=F32
            )
            if not begin:
                v = v + xa[q, h]
            if end:
                xs[q, h] = v.astype(BF16).reshape(16, 64, 256)
            else:
                xa[q, h] = v

    def far_chunk(h, pairs, end=False):
        for d, k in pairs:
            sibs[h, 1 + dist[d] * 2 + k].wait_recv()
        chunk(h, [(buf(h, d, k), n, 2 * k + n, d) for d, k in pairs for n in range(2)], False, end)

    for h in range(2):
        to_sib(h, own[h], 0)
    for h in range(2):
        sibs[h, 0].wait_recv()
        chunk(h, [(own[h], i, i, 0) for i in range(4)], True, False)
    early, late, last = ((-1, 0), (1, 1)), ((-1, 1), (1, 0)), ((2, 0), (2, 1))
    for h in range(2):
        for i, (d, k) in enumerate(early):
            first[h, i, k].wait_recv()
            cp = rcopy(buf(h, d, k).at[mine], buf(h, 2, k).at[mine], rs.at[h, 2, k], rr.at[h, 2, k], along(h, -d))
            cp.start()
            relays.append(cp)
            to_sib_far(h, d, k)
    far_chunk(0, early)
    for h in range(2):
        for i, (d, k) in enumerate(late):
            first[h, i, k].wait_recv()
            to_sib_far(h, d, k)
    far_chunk(1, early)
    far_chunk(0, late)
    for n, (h, k) in enumerate(((0, 0), (0, 1), (1, 0), (1, 1))):
        relays[n].wait_recv()
        to_sib_far(h, 2, k)
    far_chunk(1, late)
    far_chunk(0, last, True)
    far_chunk(1, last, True)

    def distance(o):
        return (1 - o // 2) * (2 - o) + (o // 2) * (9 - 3 * o)

    def send(p, o):
        d = distance(o)
        return rcopy(sb.at[p, o], rin.at[p, o], ss.at[p, o], sr.at[p, o], along(p, d))

    @pl.loop(0, 4)
    def _(o):
        d = distance(o)
        for p in range(2):
            j = ((x, y)[p] + d) % 4
            for i in range(4):
                for u in range(2):
                    e = ((j * 4 + i) if p == 0 else (i * 4 + j)) * 4 + 2 * p + u
                    r, s = ex[0, e], ex[1, e]
                    left, right = [], []
                    for q in range(3):
                        for h in range(2):
                            a = xs[q, h, r]
                            left.append(
                                jnp.concatenate([a, jnp.concatenate([a[:, 128:], -a[:, :128]], axis=1)], axis=0)
                            )
                            right.append(xs[q, h, s])
                    v = lax.dot_general(
                        jnp.concatenate(left, axis=1),
                        jnp.concatenate(right, axis=1),
                        NT,
                        preferred_element_type=F32,
                    )
                    v = jnp.concatenate([v[:64], v[64:]], axis=1)
                    sb[p, o, i, u] = v.astype(BF16)
                    sf[p, i, u] = v

            @pl.when(o < 3)
            def _():
                send(p, o).start()

    sent = []
    for p in range(2):
        total = sf[p]
        for o in range(3):
            cp = send(p, o)
            sent.append(cp)
            cp.wait_recv()
            total = total + rin[p, o].astype(F32)
        af[p] = total
        ab[p] = total.astype(BF16)
        for d in range(1, 4):
            cp = rcopy(
                ab.at[p, (cell[p] + d) % 4], qin.at[p, d - 1], qs.at[p, d - 1], qr.at[p, d - 1], cross(p, d)
            )
            cp.start()
            sent.append(cp)
    for p in range(2):
        total = af[p, cell[p]]
        for d in range(1, 4):
            sent[p * 6 + 2 + d].wait_recv()
            total = total + qin[p, d - 1].astype(F32)
        cf[2 * p : 2 * p + 2] = total
        cb[2 * p : 2 * p + 2] = total.astype(BF16)
    wc = []
    for j in range(3):
        cp = rcopy(cb.at[(zl + j + 1) % 4], zin.at[j], ws.at[j], wr.at[j], wdev[j])
        cp.start()
        wc.append(cp)
    total = cf[zl]
    for j in range(3):
        wc[j].wait_recv()
        total = total + zin[j].astype(F32)
    out[...] = total * factor
    for cps in (first, sibs):
        for cp in cps.values():
            cp.wait_send()
    for cp in pc + relays + sent + wc:
        cp.wait_send()


def fused(factor, match, ex, lists, coeff, lin):
    smem = pl.BlockSpec(memory_space=pltpu.SMEM)
    vmem = pl.BlockSpec(memory_space=pltpu.VMEM)
    hbm = pl.BlockSpec(memory_space=pl.ANY)
    dma = pltpu.SemaphoreType.DMA

    def kern(*refs):
        fused_kernel(factor, *refs)

    scratch = [pltpu.VMEM((4, 4, 4, 2, 16, 128), BF16)] * 2 + [pltpu.VMEM((4, 2, 4, 2, 16, 128), BF16)] * 12
    scratch += [
        pltpu.VMEM((145, 64, 128), BF16),
        pltpu.VMEM((3, 16, 1024, 128), BF16),
        pltpu.VMEM((3, 2, 1024, 256), F32),
        pltpu.VMEM((3, 2, 16, 64, 256), BF16),
        pltpu.VMEM((2, 4, 2, 64, 128), F32),
        pltpu.VMEM((2, 4, 4, 2, 64, 128), BF16),
        pltpu.VMEM((2, 3, 4, 2, 64, 128), BF16),
        pltpu.VMEM((2, 4, 2, 64, 128), F32),
        pltpu.VMEM((2, 4, 2, 64, 128), BF16),
        pltpu.VMEM((2, 3, 2, 64, 128), BF16),
        pltpu.VMEM((4, 64, 128), F32),
        pltpu.VMEM((4, 64, 128), BF16),
        pltpu.VMEM((3, 64, 128), BF16),
        pltpu.VMEM((3, 256), jnp.int32),
        pltpu.SMEM((4,), jnp.int32),
        pltpu.SMEM((3, 256), jnp.int32),
        dma((6,)),
    ]
    for shape in ((7, 2), (2, 3), (2, 3, 2), (2, 7), (2, 3), (2, 3), (3,)):
        scratch += [dma(shape)] * 2
    return pl.pallas_call(
        kern,
        out_shape=jax.ShapeDtypeStruct((64, 128), F32),
        in_specs=[smem] * 2 + [vmem] + [hbm] * 2,
        out_specs=vmem,
        scratch_shapes=scratch,
        compiler_params=pltpu.CompilerParams(
            collective_id=0, has_side_effects=True, vmem_limit_bytes=60 * 2**20
        ),
        name="fused",
    )(match, ex, lists, coeff, lin)


def on_device(integrals, block_lists, coeff, match, ex_blocks):
    nq, naux, occ = 3, 64, 256
    factor = -((nq * naux * occ) ** (-0.5))
    lin = integrals.reshape(144, 64, 128)
    return fused(factor, match, ex_blocks[0], block_lists[:, 0, 0], coeff, lin)[None]


def solution(mesh):
    return jax.shard_map(
        on_device,
        mesh=mesh,
        in_specs=(
            P(None, "ka", "fit", None, None, None),
            P(None, "ka", "fit", None, None),
            P("ka", None, "fit", None),
            P(),
            P("ka", None, None),
        ),
        out_specs=P("ka", "fit", None),
        check_vma=False,
    )
```

time: 1860 us -> 55.5 us (0.03)
  waiting for transfers between devices: 1710 us -> 0 us
  Pallas kernels: 0 us -> 53.8 us
  local copies, waits for them, and re-layouts: 44.9 us -> 1.38 us
  matrix products: 42.1 us -> 0 us
  between operations: 19.3 us -> 0.01 us
    all_gather x3 -> x0, waiting for transfers between devices: 991 us -> none  [on_device(): lax.all_gather(jnp.take(shards, partner, axis=0), 'fit', axis=2, tiled=True)]
    psum x1 -> x0, waiting for transfers between devices: 721 us -> none  [on_device(): whole = lax.psum(pending, 'fit')]
    pallas_call x0 -> x1, Pallas kernels: none -> 53.8 us  [fused(): pl.pallas_call(kern, out_shape=jax.ShapeDtypeStruct((64, 128), F32), in_s...]
    dot_general x12 -> x0, matrix products: 42.1 us -> none  [the longest x3 17.2 us: half_transform(): jnp.einsum('rb,bmj->rmj', onehot, prods, precision=lax.Precision.HIGHEST)]
    gather x9 -> x0, local copies, waits for them, and re-layouts: 32.4 us -> none  [the longest x3 15.4 us: half_transform(): picked = jnp.take(operands, lists[1], axis=0)]
  transfers between devices with their start and end apart: 4 -> 0, of which waited for: 4 -> 0; matrix products, arithmetic and copies ran while one was open for 3% -> 0% of each run, Pallas kernels for 0% -> 0%
where the time goes in v4:
time: 55.5 us; the launch traced here: 55.2 us
  Pallas kernels  53.8 us (97%)
  local copies, waits for them, and re-layouts  1.38 us (2%)
    pallas_call x1, Pallas kernels, fused(): pl.pallas_call(kern, out_shape=jax.ShapeDtypeStruct((64, 128), F32), in_s...  53.8 us
    unnamed x1, local copies, waits for them, and re-layouts  1.38 us

profile of v4, /device:TPU:8, one launch (start us, length us, event | category | flops | bytes accessed | tf_op | source)
XLA Modules:
  0.0 55.2 jit_solution(6868144128960783934)
XLA Ops:
  0.0 53.8 %fused.1 = f32[64,128]{1,0:T(8,128)} custom-call(s32[3,4]{1,0:T(4,128)} %refs_0_.1, s32[2,64]{1,0:T(2,128)} %bitcast.7, s32[3,2,48]{2,1,0:T(2,128)} %bitcast.6, bf16[1,2,16,256]{3,2,1,0:T(8,128)(2,1)} %refs_3_.1, bf16[144,64,128]{2,1,0:T(8,128)(2,1)} %bitcast.4), custom_call_target="tpu_custom_call" | custom-call | tf_op jit(solution)/shard_map/fused/pallas_call | solution.py:308
  53.8 1.4 %copy.7 = f32[1,64,128]{2,1,0:T(8,128)} copy(f32[1,64,128]{2,1,0:T(8,128)} %bitcast.5) | data formatting | bytes 65536

commit v5 on v4

--- a/solution.py
+++ b/solution.py
@@ -35,20 +35,26 @@
 
 
 def fused_kernel(factor, match, ex, lists, coeff, lin, out, *scratch):
-    own, far = scratch[0:2], scratch[2:14]
-    (lv, ld, xa, xs, sf, sb, rin, af, ab, qin, cf, cb, zin, table, where, idx) = scratch[14:30]
-    lsem, zs, zr, ps, pr, rs, rr, bs, br, ss, sr, qs, qr, ws, wr = scratch[30:]
+    own, far = scratch[0:2], scratch[2:10]
+    (lv, ld, xa, xs, sf, sb, rin, af, ab, qin, cf, cb, zin, table, where, idx) = scratch[10:26]
+    lsem, zs, zr, ps, pr, rs, rr, bs, br, ss, sr, qs, qr, ws, wr = scratch[26:]
+    groups = (
+        ((-1, 0), (1, 0), (-1, 1), (1, 3)),
+        ((-1, 3), (-1, 2), (1, 2), (1, 1)),
+        ((2, 0), (2, 3)),
+        ((2, 1), (2, 2)),
+    )
+    spot = {dr: (g, n) for g, drs in enumerate(groups) for n, dr in enumerate(drs)}
     zh, c, x, y, zl = place()
     z = zh * 4 + zl
     cell = (y, x)
     mine = pl.ds(c * 2, 2)
-    dist = {-1: 0, 1: 1, 2: 2}
     loads = []
     for h in range(2):
         for s in range(2):
             cp = pltpu.make_async_copy(
                 coeff.at[0, s, :, h * 128 : (h + 1) * 128],
-                own[h].at[c * 2 + zh, cell[h], zl, s],
+                own[h].at[c * 2 + zh, 0, zl, s],
                 lsem.at[h * 2 + s],
             )
             cp.start()
@@ -78,7 +84,7 @@
     zc = []
     for j in range(7):
         for h in range(2):
-            ref = own[h].at[c * 2 + zh, cell[h], zl]
+            ref = own[h].at[c * 2 + zh, 0, zl]
             cp = rcopy(ref, ref, zs.at[j, h], zr.at[j, h], zdev[j])
             cp.start()
             zc.append(cp)
@@ -111,46 +117,43 @@
     pc = []
     for d in range(1, 4):
         for h in range(2):
-            ref = own[h].at[mine, cell[h]]
-            cp = rcopy(ref, ref, ps.at[h, d - 1], pr.at[h, d - 1], cross(h, d))
+            cp = rcopy(
+                own[h].at[mine, 0], own[h].at[mine, 4 - d], ps.at[h, d - 1], pr.at[h, d - 1], cross(h, d)
+            )
             cp.start()
             pc.append(cp)
-    for cp in pc:
-        cp.wait_recv()
-
-    def buf(h, d, k):
-        return far[(h * 3 + dist[d]) * 2 + k]
-
-    first, sibs, relays = {}, {}, []
-    for s in range(2):
-        for h in range(2):
-            for i, d in enumerate((1, -1)):
-                k = s if i == 0 else 1 - s
-                cp = rcopy(
-                    own[h].at[mine, 2 * k : 2 * k + 2],
-                    buf(h, -d, k).at[mine],
-                    rs.at[h, i, k],
-                    rr.at[h, i, k],
-                    along(h, d),
-                )
-                cp.start()
-                first[h, i, k] = cp
+
+    def place_of(h, d, r):
+        g, n = spot[d, r]
+        return far[h * 4 + g].at[mine, n]
+
+    moved, sibs = {}, {}
+
+    def step(h, i, r):
+        d = (1, -1)[i]
+        cp = rcopy(own[h].at[mine, r], place_of(h, -d, r), rs.at[h, i, r], rr.at[h, i, r], along(h, d))
+        cp.start()
+        moved[h, i, r] = cp
+
+    def relay(h, i, r, n):
+        d = (1, -1)[i]
+        moved[h, i, r].wait_recv()
+        cp = rcopy(place_of(h, -d, r), place_of(h, 2, r), rs.at[h, i, n], rr.at[h, i, n], along(h, d))
+        cp.start()
+        moved[h, i, n] = cp
 
     def to_sib(h, ref, n):
         cp = rcopy(ref.at[mine], ref.at[mine], bs.at[h, n], br.at[h, n], sib)
         cp.start()
         sibs[h, n] = cp
 
-    def to_sib_far(h, d, k):
-        to_sib(h, buf(h, d, k), 1 + dist[d] * 2 + k)
-
-    def chunk(h, parts, begin, end):
+    def chunk(h, cells, begin, end):
         @pl.loop(0, 3)
         def _(q):
             pk = where[match[q, zh * 2 + c]]
             left, right = [], []
-            for ref, n, i, d in parts:
-                j = ((x, y)[h] + d + 4) % 4
+            for ref, n, d, r in cells:
+                j, i = ((x, y)[h] + d + 4) % 4, (cell[h] + r) % 4
                 left.append(ld[q, j * 4 + i] if h == 0 else ld[q, i * 4 + j])
                 re, im = (ref[pk, n, :, s].reshape(64, 128) for s in range(2))
                 right += [jnp.concatenate([re, im], axis=1), jnp.concatenate([-im, re], axis=1)]
@@ -164,83 +167,105 @@
             else:
                 xa[q, h] = v
 
-    def far_chunk(h, pairs, end=False):
-        for d, k in pairs:
-            sibs[h, 1 + dist[d] * 2 + k].wait_recv()
-        chunk(h, [(buf(h, d, k), n, 2 * k + n, d) for d, k in pairs for n in range(2)], False, end)
-
+    def far_chunk(h, g):
+        sibs[h, 1 + g].wait_recv()
+        chunk(h, [(far[h * 4 + g], n, d, r) for n, (d, r) in enumerate(groups[g])], False, g == 3)
+
+    for h in range(2):
+        step(h, 0, 0)
+        step(h, 1, 0)
+    for cp in pc:
+        cp.wait_recv()
+    for ru, rd in ((1, 3), (3, 2), (2, 1)):
+        for h in range(2):
+            step(h, 0, ru)
+            step(h, 1, rd)
     for h in range(2):
         to_sib(h, own[h], 0)
     for h in range(2):
+        relay(h, 0, 0, 4)
+    for h in range(2):
         sibs[h, 0].wait_recv()
-        chunk(h, [(own[h], i, i, 0) for i in range(4)], True, False)
-    early, late, last = ((-1, 0), (1, 1)), ((-1, 1), (1, 0)), ((2, 0), (2, 1))
-    for h in range(2):
-        for i, (d, k) in enumerate(early):
-            first[h, i, k].wait_recv()
-            cp = rcopy(buf(h, d, k).at[mine], buf(h, 2, k).at[mine], rs.at[h, 2, k], rr.at[h, 2, k], along(h, -d))
-            cp.start()
-            relays.append(cp)
-            to_sib_far(h, d, k)
-    far_chunk(0, early)
-    for h in range(2):
-        for i, (d, k) in enumerate(late):
-            first[h, i, k].wait_recv()
-            to_sib_far(h, d, k)
-    far_chunk(1, early)
-    far_chunk(0, late)
-    for n, (h, k) in enumerate(((0, 0), (0, 1), (1, 0), (1, 1))):
-        relays[n].wait_recv()
-        to_sib_far(h, 2, k)
-    far_chunk(1, late)
-    far_chunk(0, last, True)
-    far_chunk(1, last, True)
+        chunk(h, [(own[h], r, 0, r) for r in range(4)], True, False)
+    for h in range(2):
+        relay(h, 1, 3, 4)
+        relay(h, 0, 1, 5)
+        moved[h, 1, 0].wait_recv()
+        to_sib(h, far[h * 4], 1)
+    far_chunk(0, 0)
+    for h in range(2):
+        relay(h, 1, 2, 5)
+    far_chunk(1, 0)
+    for h in range(2):
+        for i, r in ((0, 3), (0, 2), (1, 1)):
+            moved[h, i, r].wait_recv()
+        to_sib(h, far[h * 4 + 1], 2)
+    far_chunk(0, 1)
+    for h in range(2):
+        for i in range(2):
+            moved[h, i, 4].wait_recv()
+        to_sib(h, far[h * 4 + 2], 3)
+    far_chunk(1, 1)
+    far_chunk(0, 2)
+    for h in range(2):
+        for i in range(2):
+            moved[h, i, 5].wait_recv()
+        to_sib(h, far[h * 4 + 3], 4)
+    far_chunk(1, 2)
+    far_chunk(0, 3)
+    far_chunk(1, 3)
 
     def distance(o):
         return (1 - o // 2) * (2 - o) + (o // 2) * (9 - 3 * o)
 
-    def send(p, o):
-        d = distance(o)
-        return rcopy(sb.at[p, o], rin.at[p, o], ss.at[p, o], sr.at[p, o], along(p, d))
+    def send(p, o, half):
+        two = pl.ds(2 * half, 2)
+        return rcopy(
+            sb.at[p, o, two], rin.at[p, o, two], ss.at[p, o, half], sr.at[p, o, half], along(p, distance(o))
+        )
 
     @pl.loop(0, 4)
     def _(o):
         d = distance(o)
-        for p in range(2):
-            j = ((x, y)[p] + d) % 4
-            for i in range(4):
-                for u in range(2):
-                    e = ((j * 4 + i) if p == 0 else (i * 4 + j)) * 4 + 2 * p + u
-                    r, s = ex[0, e], ex[1, e]
-                    left, right = [], []
-                    for q in range(3):
-                        for h in range(2):
-                            a = xs[q, h, r]
-                            left.append(
-                                jnp.concatenate([a, jnp.concatenate([a[:, 128:], -a[:, :128]], axis=1)], axis=0)
-                            )
-                            right.append(xs[q, h, s])
-                    v = lax.dot_general(
-                        jnp.concatenate(left, axis=1),
-                        jnp.concatenate(right, axis=1),
-                        NT,
-                        preferred_element_type=F32,
-                    )
-                    v = jnp.concatenate([v[:64], v[64:]], axis=1)
-                    sb[p, o, i, u] = v.astype(BF16)
-                    sf[p, i, u] = v
-
-            @pl.when(o < 3)
-            def _():
-                send(p, o).start()
+        for half in range(2):
+            for p in range(2):
+                j = ((x, y)[p] + d) % 4
+                for i in (2 * half, 2 * half + 1):
+                    for u in range(2):
+                        e = ((j * 4 + i) if p == 0 else (i * 4 + j)) * 4 + 2 * p + u
+                        r, s = ex[0, e], ex[1, e]
+                        left, right = [], []
+                        for q in range(3):
+                            for h in range(2):
+                                a = xs[q, h, r]
+                                left.append(
+                                    jnp.concatenate(
+                                        [a, jnp.concatenate([a[:, 128:], -a[:, :128]], axis=1)], axis=0
+                                    )
+                                )
+                                right.append(xs[q, h, s])
+                        v = lax.dot_general(
+                            jnp.concatenate(left, axis=1),
+                            jnp.concatenate(right, axis=1),
+                            NT,
+                            preferred_element_type=F32,
+                        )
+                        v = jnp.concatenate([v[:64], v[64:]], axis=1)
+                        sb[p, o, i, u] = v.astype(BF16)
+                        sf[p, i, u] = v
+
+                @pl.when(o < 3)
+                def _():
+                    send(p, o, half).start()
 
     sent = []
     for p in range(2):
         total = sf[p]
         for o in range(3):
-            cp = send(p, o)
-            sent.append(cp)
-            cp.wait_recv()
+            for half in range(2):
+                cp = send(p, o, half)
+                sent.append(cp)
+                cp.wait_recv()
             total = total + rin[p, o].astype(F32)
         af[p] = total
         ab[p] = total.astype(BF16)
@@ -253,7 +278,7 @@
     for p in range(2):
         total = af[p, cell[p]]
         for d in range(1, 4):
-            sent[p * 6 + 2 + d].wait_recv()
+            sent[p * 9 + 5 + d].wait_recv()
             total = total + qin[p, d - 1].astype(F32)
         cf[2 * p : 2 * p + 2] = total
         cb[2 * p : 2 * p + 2] = total.astype(BF16)
@@ -267,10 +292,10 @@
         wc[j].wait_recv()
         total = total + zin[j].astype(F32)
     out[...] = total * factor
-    for cps in (first, sibs):
+    for cps in (moved, sibs):
         for cp in cps.values():
             cp.wait_send()
-    for cp in pc + relays + sent + wc:
+    for cp in pc + sent + wc:
         cp.wait_send()
 
 
@@ -283,7 +308,9 @@
     def kern(*refs):
         fused_kernel(factor, *refs)
 
-    scratch = [pltpu.VMEM((4, 4, 4, 2, 16, 128), BF16)] * 2 + [pltpu.VMEM((4, 2, 4, 2, 16, 128), BF16)] * 12
+    scratch = [pltpu.VMEM((4, 4, 4, 2, 16, 128), BF16)] * 2 + [
+        pltpu.VMEM((4, n, 4, 2, 16, 128), BF16) for n in (4, 4, 2, 2)
+    ] * 2
     scratch += [
         pltpu.VMEM((145, 64, 128), BF16),
         pltpu.VMEM((3, 16, 1024, 128), BF16),
@@ -303,7 +330,7 @@
         pltpu.SMEM((3, 256), jnp.int32),
         dma((6,)),
     ]
-    for shape in ((7, 2), (2, 3), (2, 3, 2), (2, 7), (2, 3), (2, 3), (3,)):
+    for shape in ((7, 2), (2, 3), (2, 2, 6), (2, 5), (2, 3, 2), (2, 3), (3,)):
         scratch += [dma(shape)] * 2
     return pl.pallas_call(
         kern,

time: 55.5 us -> 58.1 us (1.047)
  Pallas kernels: 53.8 us -> 56.3 us
    pallas_call x1, Pallas kernels: 53.8 us -> 56.3 us  [fused(): pl.pallas_call(kern, out_shape=jax.ShapeDtypeStruct((64, 128), F32), in_s...]
where the time goes in v5:
time: 58.1 us; the launch traced here: 57.7 us
  Pallas kernels  56.3 us (97%)
  local copies, waits for them, and re-layouts  1.38 us (2%)
    pallas_call x1, Pallas kernels, fused(): pl.pallas_call(kern, out_shape=jax.ShapeDtypeStruct((64, 128), F32), in_s...  56.3 us
    unnamed x1, local copies, waits for them, and re-layouts  1.38 us

profile of v5, /device:TPU:8, one launch (start us, length us, event | category | flops | bytes accessed | tf_op | source)
XLA Modules:
  0.0 57.7 jit_solution(3866145001840936741)
XLA Ops:
  0.0 56.3 %fused.1 = f32[64,128]{1,0:T(8,128)} custom-call(s32[3,4]{1,0:T(4,128)} %refs_0_.1, s32[2,64]{1,0:T(2,128)} %bitcast.7, s32[3,2,48]{2,1,0:T(2,128)} %bitcast.6, bf16[1,2,16,256]{3,2,1,0:T(8,128)(2,1)} %refs_3_.1, bf16[144,64,128]{2,1,0:T(8,128)(2,1)} %bitcast.4), custom_call_target="tpu_custom_call" | custom-call | tf_op jit(solution)/shard_map/fused/pallas_call | solution.py:335
  56.3 1.4 %copy.7 = f32[1,64,128]{2,1,0:T(8,128)} copy(f32[1,64,128]{2,1,0:T(8,128)} %bitcast.5) | data formatting | bytes 65536
